TPU v7x, 256 devices: a whole 4x4x8 slice. The times are simulated.
256 devices in a mesh: own: 32 (over y, x, core), row: 8 (over z).
Axes of the slice: x: 4, y: 4, z: 8, core: 2. Of those that a mesh axis runs over, the one named last changes fastest.
Arguments:
- weights: float32 [32, 8, 128, 2048], P('own', None, 'row'), may hold values from -200 to 200
- first_moment: float32 [32, 8, 128, 2048], P('own', None, 'row'), may hold values from -20 to 20
- second_moment: float32 [32, 8, 128, 2048], P('own', None, 'row'), may hold values from 0.002 to 0.05
- gradient: bfloat16 [32, 8, 128, 2048], P('own', None, 'row'), may hold values from -0.59765625 to 0.59765625
- owner: int32 [127], replicated, may hold values from 0 to 31, as said below
Outputs:
- new_weights: float32 [32, 8, 128, 2048], P('own', None, 'row')
- new_first: float32 [32, 8, 128, 2048], P('own', None, 'row')
- new_second: float32 [32, 8, 128, 2048], P('own', None, 'row')
- low_weights: bfloat16 [32, 8, 128, 2048], P('own')
- weight_norms: float32 [14], replicated
- update_norms: float32 [14], replicated
- trust_ratios: float32 [14], replicated
Inputs may be any that keep to these rules, and one draw needn't show every extreme that they name: No owner group holds more than 8 tiles, and one holds exactly 8.
All inputs are finite; a program needn't handle non-finite values.
Results may differ from a plain program's by a relative error of at most 0.0004.
Values may be sent and summed in bfloat16 or wider, within the bound.
A program may use at most 128 MiB of HBM per device.

v0:
```python
import jax
import jax.numpy as jnp
import numpy as np
from jax import lax
from jax.sharding import PartitionSpec as P

QW = 4096
KVW = 512
NEXP = 128
FF = 768
EW = 3
TILE = 128
MATS = 14
DECAY = 0.1
STEP_SIZE = 0.05
EPSILON = 1e-06


def matrix_table():
    counts = [QW // TILE, KVW // TILE, KVW // TILE, QW // TILE, NEXP // TILE] + [FF // TILE] * (
        3 * EW
    )
    return np.repeat(np.arange(len(counts)), counts).astype(np.int32)


def slot_select(owner, owners_count, slot_count, matrices):
    tile_table = jnp.asarray(matrix_table())
    owner_hit = (owner[:, None] == jnp.arange(owners_count, dtype=jnp.int32)[None, :]).astype(
        jnp.int32
    )
    tile_rank = jnp.sum((jnp.cumsum(owner_hit, 0) - owner_hit) * owner_hit, 1)
    slot_hit = tile_rank[:, None] == jnp.arange(slot_count, dtype=jnp.int32)[None, :]
    matrix_hit = tile_table[:, None] == jnp.arange(matrices, dtype=jnp.int32)[None, :]
    owner_bool = owner_hit > 0
    joined = (
        owner_bool[:, :, None, None] & slot_hit[:, None, :, None] & matrix_hit[:, None, None, :]
    )
    return jnp.any(joined, axis=0).astype(jnp.float32)


def shards(weights, first_moment, second_moment, gradient, owner):
    slot_count = weights.shape[1]
    select_all = slot_select(owner, lax.axis_size("own"), slot_count, MATS)
    select = lax.dynamic_index_in_dim(select_all, lax.axis_index("own"), 0, keepdims=False)
    used = jnp.sum(select, 1)[None, :, None, None]
    grad_wide = gradient.astype(jnp.float32)
    moment_one = 0.5 * first_moment + 0.5 * grad_wide
    moment_two = 0.5 * second_moment + 0.5 * grad_wide * grad_wide
    direction = moment_one / (jnp.sqrt(moment_two) + EPSILON) + DECAY * weights
    weight_sq = jnp.sum(weights * weights, axis=(2, 3))[0]
    update_sq = jnp.sum(direction * direction, axis=(2, 3))[0]
    weight_part = jnp.sum(select * weight_sq[:, None], 0)
    update_part = jnp.sum(select * update_sq[:, None], 0)
    weight_total, update_total = lax.psum((weight_part, update_part), ("own", "row"))
    weight_norms = jnp.sqrt(weight_total)
    update_norms = jnp.sqrt(update_total)
    trust_ratios = weight_norms / (update_norms + EPSILON)
    slot_ratio = jnp.sum(select * trust_ratios[None, :], 1)[None, :, None, None]
    new_weights = used * (weights - STEP_SIZE * slot_ratio * direction)
    low_weights = lax.all_gather(new_weights.astype(jnp.bfloat16), "row", axis=2, tiled=True)
    new_first = used * moment_one
    new_second = used * moment_two
    return (
        new_weights,
        new_first,
        new_second,
        low_weights,
        weight_norms,
        update_norms,
        trust_ratios,
    )


def solution(mesh):
    placed = (
        P("own", None, "row", None),
        P("own", None, "row", None),
        P("own", None, "row", None),
        P("own", None, "row", None),
        P(),
    )
    return jax.shard_map(
        shards,
        mesh=mesh,
        in_specs=placed,
        out_specs=(
            P("own", None, "row", None),
            P("own", None, "row", None),
            P("own", None, "row", None),
            P("own", None, None, None),
            P(),
            P(),
            P(),
        ),
        check_vma=False,
    )
```

profile of v0, /device:TPU:1, one launch (start us, length us, event | category | flops | bytes accessed | tf_op | source)
XLA Modules:
  0.0 167.5 jit_solution(3595493397532116743)
XLA Ops:
  7.2 0.0 copy-start
  7.2 0.0 all-gather.2.cloned.1.call-start
  7.2 0.7 iota_compare_fusion.1
  8.0 0.7 fusion.4
  8.7 0.1 copy.13
  8.8 0.2 reduce_window_sum.11
  9.0 0.8 select_reduce_fusion
  9.9 7.7 %and_reduce_fusion = pred[32,8,14]{1,2,0:T(8,128)(4,1)S(1)} fusion(pred[127,14]{0,1:T(8,128)(4,1)S(1)} %iota_compare_fusion.1, pred[127,32,8]{0,2,1:T(8,128)(4,1)S(1)} %broadcast_and_fusion), kind=kLoop, calls=%fused_computation | loop fusion | flops 906752 | bytes 37874 | tf_op jit(solution)/shard_map/reduce_or | solution.py:38
  17.7 0.1 copy.14
  17.7 4.3 %multiply_reduce_fusion = (f32[8]{0:T(128)S(1)}, f32[1,8,16,2048]{3,2,1,0:T(8,128)S(1)}, f32[1,8,16,2048]{3,2,1,0:T(8,128)}, f32[1,8,16,2048]{3,2,1,0:T(8,128)}, f32[8]{0:T(128)S(1)}) fusion(f32[1,8,16,2048]{3,2,1,0:T(8,128)} %param.6, f32[1,8,16,2048]{3,2,1,0:T(8,128)} %param.8, bf16[1,8,16,2048]{3,2,1,0:T(8,128)(2,1)} %param.9, ...), kind=kLoop, calls=%fused_computation.5 | loop fusion | flops 4456432 | bytes 6815840 | tf_op jit(solution)/shard_map/reduce_sum | solution.py:51
  22.1 0.1 fusion.6
  22.2 81.4 %all-reduce = (f32[14]{0:T(128)S(1)}, f32[14]{0:T(128)S(1)}) all-reduce(f32[14]{0:T(128)S(1)} %get-tuple-element.8, f32[14]{0:T(128)S(1)} %get-tuple-element.7), channel_id=1, replica_groups=mesh['own'=32,'row'=8] {'own','row'}, use_global_device_ids=true, to_apply=%region_6.7 | all-reduce | flops 28 | bytes 224 | tf_op jit(solution)/shard_map/psum | solution.py:54
  103.6 0.5 add_divide_fusion
  104.1 0.0 copy-start.1
  104.1 0.1 fusion.7
  104.2 0.0 copy-done
  104.2 1.4 fusion.9
  105.6 0.0 all-gather.2.cloned.1.call-update
  105.7 50.2 %all-gather.2.cloned.1.call-done = bf16[1,8,128,2048]{3,2,1,0:T(8,128)(2,1)} async-done(((bf16[1,8,16,2048]{3,2,1,0:T(8,128)(2,1)}), bf16[1,8,128,2048]{3,2,1,0:T(8,128)(2,1)}) %all-gather.2.cloned.1.call-update) | async-done | bytes 4194320 | tf_op jit(solution)/shard_map/all_gather | solution.py:60
  155.8 4.8 %copy.16 = bf16[1,8,128,2048]{3,2,1,0:T(8,128)(2,1)} copy(bf16[1,8,128,2048]{3,2,1,0:T(8,128)(2,1)} %all-gather.2.cloned.1.call-done) | data formatting | bytes 8388608
  160.6 0.0 copy-done.1
  (5 shorter events, 0.1 us)
Async XLA Ops:
  7.2 97.0 %copy-start = (f32[1,8,16,2048]{3,2,1,0:T(8,128)S(1)}, f32[1,8,16,2048]{3,2,1,0:T(8,128)}, u32[]{:S(2)}) copy-start(f32[1,8,16,2048]{3,2,1,0:T(8,128)} %param.6) | copy-start | bytes 3145732
  7.2 148.6 %all-gather.2.cloned.1.call-start = ((), (), s32[]{:S(2)}) async-start(), calls=%async_computation | async-start | bytes 4718592 | tf_op jit(solution)/shard_map/all_gather | solution.py:60
  104.1 56.5 %copy-start.1 = (f32[14]{0:T(128)}, f32[14]{0:T(128)S(1)}, u32[]{:S(2)}) copy-start(f32[14]{0:T(128)S(1)} %get-tuple-element.36) | copy-start | bytes 172
Sparse Core Ops, SparseCore 0:
  105.8 50.0 all-gather.1
where the time goes:
time: 168 us; the launch traced here: 167 us
  blocking collectives  81.4 us (48%)
  waiting for transfers between devices  50.2 us (30%)
  other arithmetic  16.8 us (10%)
  between operations  14.1 us (8%)
  local copies, waits for them, and re-layouts  4.96 us (3%)
    psum x1, blocking collectives, shards(): lax.psum((weight_part, update_part), ('own', 'row'))  81.4 us
    all_gather x1, waiting for transfers between devices, shards(): lax.all_gather(new_weights.astype(jnp.bfloat16), 'row', axis=2, tiled=True)  50.2 us
    reduce_or x1, other arithmetic, slot_select(): return jnp.any(joined, axis=0).astype(jnp.float32)  7.73 us
    unnamed x5, local copies, waits for them, and re-layouts  4.8 us
    reduce_sum x1, other arithmetic, shards(): update_sq = jnp.sum(direction * direction, axis=(2, 3))[0]  4.33 us
  transfers between devices with their start and end apart: 1, of which 1 were waited for; matrix products, arithmetic and copies ran while one was open for 0% of the time, Pallas kernels for 0%

commit v1 on v0

--- a/solution.py
+++ b/solution.py
@@ -57,7 +57,20 @@
     trust_ratios = weight_norms / (update_norms + EPSILON)
     slot_ratio = jnp.sum(select * trust_ratios[None, :], 1)[None, :, None, None]
     new_weights = used * (weights - STEP_SIZE * slot_ratio * direction)
-    low_weights = lax.all_gather(new_weights.astype(jnp.bfloat16), "row", axis=2, tiled=True)
+    x = new_weights.astype(jnp.bfloat16)
+    ways, here, lap = (lax.axis_size("row"), lax.axis_index("row"), x.shape[2])
+    lengths = [n * ways if d == 2 else n for d, n in enumerate(x.shape)]
+    full = lax.dynamic_update_slice_in_dim(jnp.zeros(lengths, x.dtype), x, here * lap, axis=2)
+    going_up = going_down = x
+    for far in range(1, ways // 2 + 1):
+        going_up = lax.ppermute(going_up, "row", [(d, (d + 1) % ways) for d in range(ways)])
+        full = lax.dynamic_update_slice_in_dim(full, going_up, (here - far) % ways * lap, axis=2)
+        if 2 * far < ways:
+            going_down = lax.ppermute(going_down, "row", [(d, (d - 1) % ways) for d in range(ways)])
+            full = lax.dynamic_update_slice_in_dim(
+                full, going_down, (here + far) % ways * lap, axis=2
+            )
+    low_weights = full
     new_first = used * moment_one
     new_second = used * moment_two
     return (

time: 168 us -> 154 us (0.917); the launches traced: 167 us -> 152 us
  waiting for transfers between devices: 50.2 us -> 36.1 us
  between operations: 14.1 us -> 0.7 us
  starting transfers between devices: 0.04 us -> 8.03 us
  local copies, waits for them, and re-layouts: 4.96 us -> 8.5 us
    all_gather x1 -> x0, waiting for transfers between devices: 50.2 us -> none  [shards(): lax.all_gather(new_weights.astype(jnp.bfloat16), 'row', axis=2, tiled=True)]
    ppermute x0 -> x7, waiting for transfers between devices: none -> 36.1 us  [the longest x4 36.1 us: shards(): lax.ppermute(going_up, 'row', [(d, (d + 1) % ways) for d in range(ways)])]
    ppermute x0 -> x7, starting transfers between devices: none -> 8.03 us  [the longest x3 7.33 us: shards(): lax.ppermute(going_down, 'row', [(d, (d - 1) % ways) for d in range(ways)])]
    dynamic_update_slice x0 -> x7, local copies, waits for them, and re-layouts: none -> 5.79 us  [the longest x4 3.31 us: shards(): lax.dynamic_update_slice_in_dim(full, going_up, (here - far) % ways * lap...]
    unnamed x5 -> x4, local copies, waits for them, and re-layouts: 4.8 us -> 0.01 us
    broadcast_in_dim x0 -> x1, local copies, waits for them, and re-layouts: none -> 2.54 us  [shards(): jnp.zeros(lengths, x.dtype)]
  transfers between devices with their start and end apart: 1 -> 7, of which waited for: 1 -> 4; matrix products, arithmetic and copies ran while one was open for 0% -> 3% of each run, Pallas kernels for 0% -> 0%
where the time goes in v1:
time: 154 us; the launch traced here: 152 us
  blocking collectives  81.4 us (53%)
  waiting for transfers between devices  36.1 us (23%)
  other arithmetic  16.8 us (11%)
  local copies, waits for them, and re-layouts  8.5 us (6%)
  starting transfers between devices  8.03 us (5%)
    psum x1, blocking collectives, shards(): lax.psum((weight_part, update_part), ('own', 'row'))  81.4 us
    ppermute x4, waiting for transfers between devices, shards(): lax.ppermute(going_up, 'row', [(d, (d + 1) % ways) for d in range(ways)])  36.1 us
    reduce_or x1, other arithmetic, slot_select(): return jnp.any(joined, axis=0).astype(jnp.float32)  7.73 us
    ppermute x3, starting transfers between devices, shards(): lax.ppermute(going_down, 'row', [(d, (d - 1) % ways) for d in range(ways)])  7.33 us
    reduce_sum x1, other arithmetic, shards(): update_sq = jnp.sum(direction * direction, axis=(2, 3))[0]  4.42 us
    dynamic_update_slice x4, local copies, waits for them, and re-layouts, shards(): lax.dynamic_update_slice_in_dim(full, going_up, (here - far) % ways * lap...  3.31 us
  transfers between devices with their start and end apart: 7, of which 4 were waited for; matrix products, arithmetic and copies ran while one was open for 3% of the time, Pallas kernels for 0%

profile of v1, /device:TPU:1, one launch (start us, length us, event | category | flops | bytes accessed | tf_op | source)
XLA Modules:
  0.0 151.5 jit_solution(8885638197208512315)
XLA Ops:
  0.6 0.7 fusion.4
  1.4 0.2 reduce_window_sum.11
  1.6 0.8 select_reduce_fusion
  2.4 0.1 copy.13
  2.5 0.7 iota_compare_fusion.1
  3.2 7.7 %and_reduce_fusion = pred[32,8,14]{1,2,0:T(8,128)(4,1)S(1)} fusion(pred[127,14]{0,1:T(8,128)(4,1)S(1)} %iota_compare_fusion.1, pred[127,32,8]{0,2,1:T(8,128)(4,1)S(1)} %broadcast_and_fusion), kind=kLoop, calls=%fused_computation | loop fusion | flops 906752 | bytes 37874 | tf_op jit(solution)/shard_map/reduce_or | solution.py:38
  11.0 0.1 copy.14
  11.1 0.0 copy-start
  11.1 4.4 %multiply_reduce_fusion = (f32[8]{0:T(128)S(1)}, f32[1,8,16,2048]{3,2,1,0:T(8,128)S(1)}, f32[1,8,16,2048]{3,2,1,0:T(8,128)}, f32[1,8,16,2048]{3,2,1,0:T(8,128)}, f32[8]{0:T(128)S(1)}) fusion(f32[1,8,16,2048]{3,2,1,0:T(8,128)} %param.6, f32[1,8,16,2048]{3,2,1,0:T(8,128)} %param.8, bf16[1,8,16,2048]{3,2,1,0:T(8,128)(2,1)} %param.9, ...), kind=kLoop, calls=%fused_computation.5 | loop fusion | flops 4456432 | bytes 6815840 | tf_op jit(solution)/shard_map/reduce_sum | solution.py:51
  15.5 0.1 fusion.6
  15.6 81.4 %all-reduce = (f32[14]{0:T(128)S(1)}, f32[14]{0:T(128)S(1)}) all-reduce(f32[14]{0:T(128)S(1)} %get-tuple-element.8, f32[14]{0:T(128)S(1)} %get-tuple-element.7), channel_id=1, replica_groups=mesh['own'=32,'row'=8] {'own','row'}, use_global_device_ids=true, to_apply=%region_6.7 | all-reduce | flops 28 | bytes 224 | tf_op jit(solution)/shard_map/psum | solution.py:54
  97.0 0.5 add_divide_fusion
  97.5 0.0 copy-start.1
  97.5 0.1 fusion.7
  97.6 2.5 %broadcast_in_dim.2 = bf16[1,8,128,2048]{3,2,1,0:T(8,128)(2,1)} broadcast(bf16[]{:T(256)} %constant.80.clone.1), dimensions={} | broadcast | bytes 4194306 | tf_op jit(solution)/shard_map/broadcast_in_dim | solution.py:63
  100.2 0.0 copy-done
  100.2 1.4 constant_dynamic-update-slice_fusion.7
  101.6 0.0 copy-done.1
  101.6 0.7 collective-permute-start
  102.3 2.0 %collective-permute-start.1 = (bf16[1,8,16,2048]{3,2,1,0:T(8,128)(2,1)S(1)}, bf16[1,8,16,2048]{3,2,1,0:T(8,128)(2,1)S(1)}, u32[]{:S(2)}, u32[]{:S(2)}) collective-permute-start(bf16[1,8,16,2048]{3,2,1,0:T(8,128)(2,1)S(1)} %get-tuple-element.12), channel_id=1, source_target_pairs={{0,7},{1,0},{2,1},{3,2},{4,3},{5,4},{6,5},{7,6},{8,15},{9,8},{10,9... | collective-permute-start | bytes 1572872 | tf_op jit(solution)/shard_map/ppermute | solution.py:69
  104.2 11.0 %collective-permute-done = bf16[1,8,16,2048]{3,2,1,0:T(8,128)(2,1)S(1)} collective-permute-done((bf16[1,8,16,2048]{3,2,1,0:T(8,128)(2,1)S(1)}, bf16[1,8,16,2048]{3,2,1,0:T(8,128)(2,1)S(1)}, u32[]{:S(2)}, u32[]{:S(2)}) %collective-permute-start) | collective-permute-done | bytes 524320 | tf_op jit(solution)/shard_map/ppermute | solution.py:66
  115.2 0.0 collective-permute-start.2
  115.2 0.0 collective-permute-done.1
  115.2 2.7 %collective-permute-start.3 = (bf16[1,8,16,2048]{3,2,1,0:T(8,128)(2,1)S(1)}, bf16[1,8,16,2048]{3,2,1,0:T(8,128)(2,1)S(1)}, u32[]{:S(2)}, u32[]{:S(2)}) collective-permute-start(bf16[1,8,16,2048]{3,2,1,0:T(8,128)(2,1)S(1)} %collective-permute-done.1), channel_id=1, source_target_pairs={{0,7},{1,0},{2,1},{3,2},{4,3},{5,4},{6,5},{7,6},{8,15},{9,8},{10,9... | collective-permute-start | bytes 1572872 | tf_op jit(solution)/shard_map/ppermute | solution.py:69
  117.9 10.1 %collective-permute-done.2 = bf16[1,8,16,2048]{3,2,1,0:T(8,128)(2,1)S(1)} collective-permute-done((bf16[1,8,16,2048]{3,2,1,0:T(8,128)(2,1)S(1)}, bf16[1,8,16,2048]{3,2,1,0:T(8,128)(2,1)S(1)}, u32[]{:S(2)}, u32[]{:S(2)}) %collective-permute-start.2) | collective-permute-done | bytes 524320 | tf_op jit(solution)/shard_map/ppermute | solution.py:66
  128.0 0.0 collective-permute-start.4
  128.0 0.8 constant_dynamic-update-slice_fusion.6
  128.8 0.8 constant_dynamic-update-slice_fusion.5
  129.6 0.0 collective-permute-done.3
  129.6 2.7 %collective-permute-start.5 = (bf16[1,8,16,2048]{3,2,1,0:T(8,128)(2,1)S(1)}, bf16[1,8,16,2048]{3,2,1,0:T(8,128)(2,1)S(1)}, u32[]{:S(2)}, u32[]{:S(2)}) collective-permute-start(bf16[1,8,16,2048]{3,2,1,0:T(8,128)(2,1)S(1)} %collective-permute-done.3), channel_id=1, source_target_pairs={{0,7},{1,0},{2,1},{3,2},{4,3},{5,4},{6,5},{7,6},{8,15},{9,8},{10,9... | collective-permute-start | bytes 1572872 | tf_op jit(solution)/shard_map/ppermute | solution.py:69
  132.3 0.8 constant_dynamic-update-slice_fusion.4
  133.1 6.7 %collective-permute-done.4 = bf16[1,8,16,2048]{3,2,1,0:T(8,128)(2,1)S(1)} collective-permute-done((bf16[1,8,16,2048]{3,2,1,0:T(8,128)(2,1)S(1)}, bf16[1,8,16,2048]{3,2,1,0:T(8,128)(2,1)S(1)}, u32[]{:S(2)}, u32[]{:S(2)}) %collective-permute-start.4) | collective-permute-done | bytes 524320 | tf_op jit(solution)/shard_map/ppermute | solution.py:66
  139.8 0.0 collective-permute-start.6
  139.8 0.8 constant_dynamic-update-slice_fusion.3
  140.6 0.8 constant_dynamic-update-slice_fusion.2
  141.4 0.0 collective-permute-done.5
  141.5 0.8 constant_dynamic-update-slice_fusion.1
  142.3 8.4 %collective-permute-done.6 = bf16[1,8,16,2048]{3,2,1,0:T(8,128)(2,1)S(1)} collective-permute-done((bf16[1,8,16,2048]{3,2,1,0:T(8,128)(2,1)S(1)}, bf16[1,8,16,2048]{3,2,1,0:T(8,128)(2,1)S(1)}, u32[]{:S(2)}, u32[]{:S(2)}) %collective-permute-start.6) | collective-permute-done | bytes 524320 | tf_op jit(solution)/shard_map/ppermute | solution.py:66
  150.7 0.8 constant_dynamic-update-slice_fusion
  (5 shorter events, 0.1 us)
Async XLA Ops:
  11.1 89.1 %copy-start = (f32[1,8,16,2048]{3,2,1,0:T(8,128)S(1)}, f32[1,8,16,2048]{3,2,1,0:T(8,128)}, u32[]{:S(2)}) copy-start(f32[1,8,16,2048]{3,2,1,0:T(8,128)} %param.6) | copy-start | bytes 3145732
  97.5 4.1 %copy-start.1 = (f32[14]{0:T(128)}, f32[14]{0:T(128)S(1)}, u32[]{:S(2)}) copy-start(f32[14]{0:T(128)S(1)} %get-tuple-element.14) | copy-start | bytes 172
  101.6 13.7 %collective-permute-start = (bf16[1,8,16,2048]{3,2,1,0:T(8,128)(2,1)S(1)}, bf16[1,8,16,2048]{3,2,1,0:T(8,128)(2,1)S(1)}, u32[]{:S(2)}, u32[]{:S(2)}) collective-permute-start(bf16[1,8,16,2048]{3,2,1,0:T(8,128)(2,1)S(1)} %get-tuple-element.12), channel_id=1, source_target_pairs={{0,1},{1,2},{2,3},{3,4},{4,5},{5,6},{6,7},{7,0},{8,9},{9,10},{10,1... | collective-permute-start | bytes 1572872 | tf_op jit(solution)/shard_map/ppermute | solution.py:66
  102.3 13.0 %collective-permute-start.1 = (bf16[1,8,16,2048]{3,2,1,0:T(8,128)(2,1)S(1)}, bf16[1,8,16,2048]{3,2,1,0:T(8,128)(2,1)S(1)}, u32[]{:S(2)}, u32[]{:S(2)}) collective-permute-start(bf16[1,8,16,2048]{3,2,1,0:T(8,128)(2,1)S(1)} %get-tuple-element.12), channel_id=1, source_target_pairs={{0,7},{1,0},{2,1},{3,2},{4,3},{5,4},{6,5},{7,6},{8,15},{9,8},{10,9... | collective-permute-start | bytes 1572872 | tf_op jit(solution)/shard_map/ppermute | solution.py:69
  115.2 12.7 %collective-permute-start.2 = (bf16[1,8,16,2048]{3,2,1,0:T(8,128)(2,1)S(1)}, bf16[1,8,16,2048]{3,2,1,0:T(8,128)(2,1)S(1)}, u32[]{:S(2)}, u32[]{:S(2)}) collective-permute-start(bf16[1,8,16,2048]{3,2,1,0:T(8,128)(2,1)S(1)} %collective-permute-done), channel_id=1, source_target_pairs={{0,1},{1,2},{2,3},{3,4},{4,5},{5,6},{6,7},{7,0},{8,9},{9,10},{10,1... | collective-permute-start | bytes 1572872 | tf_op jit(solution)/shard_map/ppermute | solution.py:66
  115.2 14.4 %collective-permute-start.3 = (bf16[1,8,16,2048]{3,2,1,0:T(8,128)(2,1)S(1)}, bf16[1,8,16,2048]{3,2,1,0:T(8,128)(2,1)S(1)}, u32[]{:S(2)}, u32[]{:S(2)}) collective-permute-start(bf16[1,8,16,2048]{3,2,1,0:T(8,128)(2,1)S(1)} %collective-permute-done.1), channel_id=1, source_target_pairs={{0,7},{1,0},{2,1},{3,2},{4,3},{5,4},{6,5},{7,6},{8,15},{9,8},{10,9... | collective-permute-start | bytes 1572872 | tf_op jit(solution)/shard_map/ppermute | solution.py:69
  128.0 11.8 %collective-permute-start.4 = (bf16[1,8,16,2048]{3,2,1,0:T(8,128)(2,1)S(1)}, bf16[1,8,16,2048]{3,2,1,0:T(8,128)(2,1)S(1)}, u32[]{:S(2)}, u32[]{:S(2)}) collective-permute-start(bf16[1,8,16,2048]{3,2,1,0:T(8,128)(2,1)S(1)} %collective-permute-done.2), channel_id=1, source_target_pairs={{0,1},{1,2},{2,3},{3,4},{4,5},{5,6},{6,7},{7,0},{8,9},{9,10},{10,1... | collective-permute-start | bytes 1572872 | tf_op jit(solution)/shard_map/ppermute | solution.py:66
  129.6 11.8 %collective-permute-start.5 = (bf16[1,8,16,2048]{3,2,1,0:T(8,128)(2,1)S(1)}, bf16[1,8,16,2048]{3,2,1,0:T(8,128)(2,1)S(1)}, u32[]{:S(2)}, u32[]{:S(2)}) collective-permute-start(bf16[1,8,16,2048]{3,2,1,0:T(8,128)(2,1)S(1)} %collective-permute-done.3), channel_id=1, source_target_pairs={{0,7},{1,0},{2,1},{3,2},{4,3},{5,4},{6,5},{7,6},{8,15},{9,8},{10,9... | collective-permute-start | bytes 1572872 | tf_op jit(solution)/shard_map/ppermute | solution.py:69
  139.8 10.9 %collective-permute-start.6 = (bf16[1,8,16,2048]{3,2,1,0:T(8,128)(2,1)S(1)}, bf16[1,8,16,2048]{3,2,1,0:T(8,128)(2,1)S(1)}, u32[]{:S(2)}, u32[]{:S(2)}) collective-permute-start(bf16[1,8,16,2048]{3,2,1,0:T(8,128)(2,1)S(1)} %collective-permute-done.4), channel_id=1, source_target_pairs={{0,1},{1,2},{2,3},{3,4},{4,5},{5,6},{6,7},{7,0},{8,9},{9,10},{10,1... | collective-permute-start | bytes 1572872 | tf_op jit(solution)/shard_map/ppermute | solution.py:66
